TPU v7x, 256 devices: a whole 4x4x8 slice. The times are simulated.
256 devices in a mesh: grp: 2 (over z_lo), gx: 64 (over x, z_hi, y), gz: 2 (over core).
Axes of the slice: x: 4, y: 4, z: 8 (z_hi: 4, z_lo: 2; z = z_hi * 2 + z_lo), core: 2. Of those that a mesh axis runs over, the one named last changes fastest.
Arguments:
- fields: float32 [4, 2, 4, 4096, 1024], P(None, 'grp', None, 'gx', 'gz'), may hold values from -4 to 4
- buoyancy: float32 [2, 4, 4096, 1024], P('grp', None, 'gx', 'gz'), may hold values from 0.3 to 0.9
- stiffness: float32 [2, 4, 4096, 1024], P('grp', None, 'gx', 'gz'), may hold values from 0.2 to 0.7
- stress_zero: float32 [4096, 1024], P('gx', 'gz'), may hold values from -5 to 5
- direct_effect: float32 [4096, 1024], P('gx', 'gz'), may hold values from 1 to 8
- log_state: float32 [4096, 1024], P('gx', 'gz'), may hold values from -2 to 2
- kernel: float32 [16, 1024, 4096], P(None, ('grp', 'gx', 'gz')), may hold values from -2 to 2
- history: float32 [16, 1024, 2, 4096], P(None, ('grp', 'gx', 'gz')), may hold values from -5 to 5
- truncation: int32 [1024, 4096], P(('grp', 'gx', 'gz')), may hold values from 1 to 16
Outputs:
- fields_next: float32 [4, 2, 4, 4096, 1024], P(None, 'grp', None, 'gx', 'gz')
- state_next: float32 [4096, 1024], P('gx', 'gz')
- spectra_new: float32 [4, 1024, 2, 4096], P(None, ('grp', 'gx', 'gz'))
All inputs are finite; a program needn't handle non-finite values.
Results may differ from a plain program's by a relative error of at most 0.0003.
Values sent between devices are 32-bit elements; how exact they have to be, the bound alone decides.
A program may use at most 128 MiB of HBM per device.

v0:
```python
import math
import jax
import jax.numpy as jnp
from jax import lax
from jax.sharding import PartitionSpec as P

NSTEP = 4
NEWTON = 4
FACE_NEAR = 9.0 / 8.0
FACE_FAR = 1.0 / 24.0
DAMPING = 1.0
FULL_PRECISION = lax.Precision.HIGHEST


def extended(cells, sides, width):
    for axis, dim in sides:
        count = lax.axis_size(axis)
        ends = count - 1
        head = lax.slice_in_dim(cells, 0, width, axis=dim)
        tail = lax.slice_in_dim(cells, cells.shape[dim] - width, cells.shape[dim], axis=dim)
        cells = jnp.concatenate(
            [
                lax.ppermute(tail, axis, [(i, (i + 1) % count) for i in range(ends)]),
                cells,
                lax.ppermute(head, axis, [((i + 1) % count, i) for i in range(ends)]),
            ],
            axis=dim,
        )
    return cells


def from_partner(x, axis, stride):
    return lax.ppermute(x, axis, [(i, i ^ 1 << stride) for i in range(lax.axis_size(axis))])


def stencil(values, axis_index, pad_before, pad_after):
    widths = [(0, 0)] * values.ndim
    widths[axis_index] = (pad_before, pad_after)
    padded = jnp.pad(values, widths)
    length = values.shape[axis_index]

    def window(offset):
        return lax.slice_in_dim(padded, offset, offset + length, axis=axis_index)

    return FACE_NEAR * (window(2) - window(1)) - FACE_FAR * (window(3) - window(0))


def margin_stencil(padded, axis_index, length, lead_cells):

    def window(offset):
        return lax.slice_in_dim(
            padded, lead_cells + offset, lead_cells + offset + length, axis=axis_index
        )

    return FACE_NEAR * (window(2) - window(1)) - FACE_FAR * (window(3) - window(0))


def inverse_sinh(scaled):
    magnitude = jnp.abs(scaled)
    positive = jnp.log(magnitude + jnp.sqrt(1.0 + magnitude * magnitude))
    return jnp.where(scaled < 0.0, -positive, positive)


def friction(loading, direct_effect, log_state, initial):
    factor = jnp.exp(log_state)
    slip_rate = initial
    for repeat in range(NEWTON):
        scaled = slip_rate * factor
        misfit = direct_effect * inverse_sinh(scaled) + DAMPING * slip_rate - loading
        slope_total = direct_effect * factor / jnp.sqrt(1.0 + scaled * scaled) + DAMPING
        slip_rate = slip_rate - misfit / slope_total
    return slip_rate


def phase_table(first_index, second_index, length, direction):
    turn_count = first_index * second_index % length
    angle_value = turn_count.astype(jnp.float32) * (2.0 * math.pi / length)
    return (jnp.cos(angle_value), direction * jnp.sin(angle_value))


def complex_apply(real_part, imag_part, cos_table, sin_table, formula):
    real_cos = jnp.einsum(formula, real_part, cos_table, precision=FULL_PRECISION)
    imag_sin = jnp.einsum(formula, imag_part, sin_table, precision=FULL_PRECISION)
    real_sin = jnp.einsum(formula, real_part, sin_table, precision=FULL_PRECISION)
    imag_cos = jnp.einsum(formula, imag_part, cos_table, precision=FULL_PRECISION)
    return (real_cos - imag_sin, real_sin + imag_cos)


def strike_forward(values, outer_count, inner_count):
    planes_count = values.shape[0]
    total_count = outer_count * inner_count
    real_part = values[:, 0].reshape(planes_count, outer_count, inner_count)
    imag_part = values[:, 1].reshape(planes_count, outer_count, inner_count)
    outer_iota = jnp.arange(outer_count, dtype=jnp.int32)
    inner_iota = jnp.arange(inner_count, dtype=jnp.int32)
    cos_table, sin_table = phase_table(outer_iota[:, None], outer_iota[None, :], outer_count, -1.0)
    real_part, imag_part = complex_apply(real_part, imag_part, cos_table, sin_table, "rab,ak->rkb")
    cos_table, sin_table = phase_table(outer_iota[:, None], inner_iota[None, :], total_count, -1.0)
    real_part, imag_part = (
        real_part * cos_table - imag_part * sin_table,
        real_part * sin_table + imag_part * cos_table,
    )
    cos_table, sin_table = phase_table(inner_iota[:, None], inner_iota[None, :], inner_count, -1.0)
    real_part, imag_part = complex_apply(real_part, imag_part, cos_table, sin_table, "rkb,bm->rmk")
    return jnp.stack(
        [
            real_part.reshape(planes_count, total_count),
            imag_part.reshape(planes_count, total_count),
        ],
        axis=1,
    )


def strike_inverse(values, outer_count, inner_count):
    planes_count = values.shape[0]
    total_count = outer_count * inner_count
    real_part = values[:, 0].reshape(planes_count, inner_count, outer_count)
    imag_part = values[:, 1].reshape(planes_count, inner_count, outer_count)
    outer_iota = jnp.arange(outer_count, dtype=jnp.int32)
    inner_iota = jnp.arange(inner_count, dtype=jnp.int32)
    cos_table, sin_table = phase_table(inner_iota[:, None], inner_iota[None, :], inner_count, 1.0)
    real_part, imag_part = complex_apply(real_part, imag_part, cos_table, sin_table, "rmk,mb->rkb")
    cos_table, sin_table = phase_table(outer_iota[:, None], inner_iota[None, :], total_count, 1.0)
    real_part, imag_part = (
        real_part * cos_table - imag_part * sin_table,
        real_part * sin_table + imag_part * cos_table,
    )
    cos_table, sin_table = phase_table(outer_iota[:, None], outer_iota[None, :], outer_count, 1.0)
    real_part, imag_part = complex_apply(real_part, imag_part, cos_table, sin_table, "rkb,ka->rab")
    return jnp.stack(
        [
            real_part.reshape(planes_count, total_count),
            imag_part.reshape(planes_count, total_count),
        ],
        axis=1,
    )


def per_device(
    fields, buoyancy, stiffness, stress_zero, direct_effect, log_state, kernel, history, truncation
):
    side_index = lax.axis_index("grp")
    on_plus = side_index == 1
    depth_index = lax.axis_index("gz")
    strike_devices = lax.axis_size("gx")
    depth_devices = lax.axis_size("gz")
    velocity = fields[0]
    normal_stress = fields[1]
    shear_stress = fields[2:4]
    strike_rows = velocity.shape[2]
    depth_cols = velocity.shape[3]
    modes_dev = history.shape[1]
    strike_total = history.shape[3]
    depth_total = depth_cols * depth_devices
    mode_rows = strike_devices * modes_dev
    scale_back = 1.0 / math.sqrt(strike_total * depth_total)
    lag_number = lax.broadcasted_iota(jnp.int32, kernel.shape, 0)
    weights = jnp.where(lag_number < truncation[None], kernel, jnp.zeros_like(kernel))

    def mode_numbers(row_index, depth_part):
        return (
            (side_index * strike_devices + row_index // modes_dev) * depth_devices + depth_part
        ) * modes_dev + row_index % modes_dev

    own_modes = mode_numbers(jnp.arange(mode_rows, dtype=jnp.int32), depth_index)
    depth_iota = jnp.arange(depth_total, dtype=jnp.int32)
    back_cos, back_sin = phase_table(own_modes[:, None], depth_iota[None, :], depth_total, 1.0)
    lagged = history
    spectra = []
    for step_number in range(NSTEP):
        summed = jnp.sum(weights[:, :, None, :] * lagged, axis=0)
        in_space = strike_inverse(summed, strike_devices, strike_rows)
        by_rows = lax.all_to_all(in_space, "gx", split_axis=2, concat_axis=0, tiled=True)
        partial_value = jnp.einsum(
            "jy,jz->yz", by_rows[:, 0], back_cos, precision=FULL_PRECISION
        ) - jnp.einsum("jy,jz->yz", by_rows[:, 1], back_sin, precision=FULL_PRECISION)
        own_depth = lax.psum_scatter(partial_value, "gz", scatter_dimension=1, tiled=True)
        relief = lax.psum(own_depth, "grp") * scale_back
        padded = extended(velocity, (("gx", 2), ("gz", 3)), 2)
        normal_stress = normal_stress + stiffness * stencil(velocity, 1, 2, 1)
        strike_grad = margin_stencil(padded[:, :, :, 2 : 2 + depth_cols], 2, strike_rows, 1)
        depth_grad = margin_stencil(padded[:, :, 2 : 2 + strike_rows, :], 3, depth_cols, 1)
        shear_stress = shear_stress + stiffness * jnp.stack([strike_grad, depth_grad])
        near_plane = velocity[0, 0]
        far_plane = from_partner(near_plane, "grp", 0)
        velocity_plus = jnp.where(on_plus, near_plane, far_plane)
        velocity_minus = jnp.where(on_plus, far_plane, near_plane)
        slip_guess = velocity_plus - velocity_minus
        loading = stress_zero + relief + DAMPING * slip_guess
        slip_rate = friction(loading, direct_effect, log_state, slip_guess)
        traction = loading - DAMPING * slip_rate
        log_state = 0.75 * log_state - 0.2 * jnp.log(1.0 + slip_rate * slip_rate) + 0.1
        normal_stress = normal_stress.at[0, 0].set(jnp.where(on_plus, traction, -traction))
        shear_rim = extended(shear_stress, (("gx", 3), ("gz", 4)), 2)
        strike_div = margin_stencil(shear_rim[0][:, :, :, 2 : 2 + depth_cols], 2, strike_rows, 0)
        depth_div = margin_stencil(shear_rim[1][:, :, 2 : 2 + strike_rows, :], 3, depth_cols, 0)
        velocity = velocity + buoyancy * (stencil(normal_stress, 1, 1, 2) + strike_div + depth_div)
        term_index = jnp.arange(mode_rows * lax.axis_size("gz"), dtype=jnp.int32)
        term_modes = mode_numbers(term_index % mode_rows, term_index // mode_rows)
        depth_here = depth_index * depth_cols + jnp.arange(depth_cols, dtype=jnp.int32)
        cos_part, sin_part = phase_table(
            term_modes[:, None], depth_here[None, :], depth_total, -1.0
        )
        real_term = jnp.einsum("jz,yz->jy", cos_part, slip_rate, precision=FULL_PRECISION)
        imag_term = jnp.einsum("jz,yz->jy", sin_part, slip_rate, precision=FULL_PRECISION)
        by_modes = lax.psum_scatter(
            jnp.stack([real_term, imag_term], axis=1), "gz", scatter_dimension=0, tiled=True
        )
        spread = lax.all_to_all(by_modes, "gx", split_axis=0, concat_axis=2, tiled=True)
        fresh_modes = strike_forward(spread, strike_devices, strike_rows) * scale_back
        spectra.append(fresh_modes)
        lagged = jnp.concatenate([fresh_modes[None], lagged[:-1]], axis=0)
    return (
        jnp.stack([velocity, normal_stress, shear_stress[0], shear_stress[1]]),
        log_state,
        jnp.stack(spectra),
    )


def solution(mesh):
    return jax.shard_map(
        per_device,
        mesh=mesh,
        in_specs=(
            P(None, "grp", None, "gx", "gz"),
            P("grp", None, "gx", "gz"),
            P("grp", None, "gx", "gz"),
            P("gx", "gz"),
            P("gx", "gz"),
            P("gx", "gz"),
            P(None, ("grp", "gx", "gz"), None),
            P(None, ("grp", "gx", "gz"), None, None),
            P(("grp", "gx", "gz"), None),
        ),
        out_specs=(
            P(None, "grp", None, "gx", "gz"),
            P("gx", "gz"),
            P(None, ("grp", "gx", "gz"), None, None),
        ),
        check_vma=False,
    )
```

profile of v0, /device:TPU:1, one launch (start us, length us, event | category | flops | bytes accessed | tf_op | source)
XLA Modules:
  0.0 803.6 jit_solution(6997939394833421156)
XLA Ops:
  9.7 4.6 collective-permute-start.2
  22.0 4.4 copy.238
  26.4 7.4 reshape.589
  33.9 18.6 %all-to-all-start = ((f32[64,1,512]{2,1,0:T(1,128)}), f32[64,1,512]{2,1,0:T(1,128)S(1)}, u32[]{:S(2)}, u32[]{:S(2)}) async-start(f32[64,1,512]{2,1,0:T(1,128)} %reshape.589), calls=%async_computation | async-start | bytes 262144 | tf_op jit(solution)/shard_map/all_to_all | solution.py:173
  69.9 7.9 reshape.590
  77.8 5.4 copy.332
  83.3 4.6 fusion.195
  88.0 5.4 convolution_subtract_fusion.3
  94.1 10.1 %collective-permute-start = (f32[64,512]{1,0:T(8,128)}, f32[64,512]{1,0:T(8,128)}, u32[]{:S(2)}, u32[]{:S(2)}) collective-permute-start(f32[64,512]{1,0:T(8,128)} %slice_bitcast_fusion.24), channel_id=1, source_target_pairs={{0,128},{128,0},{1,129},{129,1},{2,130},{130,2},{3,131},{131,3},{4... | collective-permute-start | bytes 393224 | tf_op jit(solution)/shard_map/ppermute | solution.py:33
  117.8 33.4 %all-reduce.13.cloned.1.call-done = f32[64,512]{1,0:T(8,128)} async-done(((f32[64,512]{1,0:T(8,128)}), f32[64,512]{1,0:T(8,128)}) %all-reduce.13.cloned.1.call-update) | async-done | bytes 131088 | tf_op jit(solution)/shard_map/psum | solution.py:178
  153.4 5.0 convolution_bitcast_fusion.6
  158.4 4.9 convolution_bitcast_fusion.7
  164.0 4.7 fusion.70
  175.6 5.2 collective-permute-start.12
  187.7 17.2 %all-to-all-start.1 = ((f32[64,1,512]{2,1,0:T(1,128)}), f32[64,1,512]{2,1,0:T(1,128)S(1)}, u32[]{:S(2)}, u32[]{:S(2)}) async-start(f32[64,1,512]{2,1,0:T(1,128)} %reshape.591), calls=%async_computation.3 | async-start | bytes 262144 | tf_op jit(solution)/shard_map/all_to_all | solution.py:209
  208.3 8.1 %all-to-all-done.1 = f32[64,1,512]{2,1,0:T(1,128)S(1)} async-done(((f32[64,1,512]{2,1,0:T(1,128)}), f32[64,1,512]{2,1,0:T(1,128)S(1)}, u32[]{:S(2)}, u32[]{:S(2)}) %all-to-all-start.1) | async-done | bytes 131104 | tf_op jit(solution)/shard_map/all_to_all | solution.py:209
  256.2 4.4 copy.256
  260.6 7.4 reshape.593
  268.0 4.6 all-to-all-start.2
  279.8 4.3 all-to-all-done.2
  285.0 8.0 reshape.594
  293.0 5.4 copy.337
  298.5 4.6 fusion.193
  303.1 5.4 convolution_subtract_fusion.2
  311.2 6.3 collective-permute-start.17
  321.3 4.2 reduce-scatter.13.cloned.1.call-done
  328.1 32.7 %all-reduce.15.cloned.1.call-done = f32[64,512]{1,0:T(8,128)} async-done(((f32[64,512]{1,0:T(8,128)}), f32[64,512]{1,0:T(8,128)}) %all-reduce.15.cloned.1.call-update) | async-done | bytes 131088 | tf_op jit(solution)/shard_map/psum | solution.py:178
  362.9 5.0 convolution_bitcast_fusion.4
  367.9 4.9 convolution_bitcast_fusion.5
  380.9 4.4 collective-permute-start.21
  391.2 7.4 reduce-scatter.15.cloned.1.call-done
  402.2 12.6 %all-to-all-start.3 = ((f32[64,1,512]{2,1,0:T(1,128)}), f32[64,1,512]{2,1,0:T(1,128)}, u32[]{:S(2)}, u32[]{:S(2)}) async-start(f32[64,1,512]{2,1,0:T(1,128)} %reshape.595), calls=%async_computation.7 | async-start | bytes 262144 | tf_op jit(solution)/shard_map/all_to_all | solution.py:209
  418.1 8.6 %all-to-all-done.3 = f32[64,1,512]{2,1,0:T(1,128)} async-done(((f32[64,1,512]{2,1,0:T(1,128)}), f32[64,1,512]{2,1,0:T(1,128)}, u32[]{:S(2)}, u32[]{:S(2)}) %all-to-all-start.3) | async-done | bytes 131104 | tf_op jit(solution)/shard_map/all_to_all | solution.py:209
  450.4 4.4 copy.272
  454.8 7.5 reshape.597
  462.3 5.5 all-to-all-start.4
  480.8 8.3 %reshape.598 = f32[4096,2,4]{2,1,0:T(2,128)} reshape(f32[64,512]{1,0:T(8,128)S(1)} %reduce.44) | data formatting | bytes 262144
  489.1 5.4 copy.342
  494.7 4.6 fusion.191
  499.3 5.4 convolution_subtract_fusion.1
  507.4 4.6 collective-permute-start.26
  516.1 4.9 reduce-scatter.17.cloned.1.call-done
  523.7 32.8 %all-reduce.17.cloned.1.call-done = f32[64,512]{1,0:T(8,128)} async-done(((f32[64,512]{1,0:T(8,128)}), f32[64,512]{1,0:T(8,128)}) %all-reduce.17.cloned.1.call-update) | async-done | bytes 131088 | tf_op jit(solution)/shard_map/psum | solution.py:178
  558.7 5.0 convolution_bitcast_fusion.2
  563.7 4.9 convolution_bitcast_fusion.3
  569.3 4.7 fusion.102
  581.2 5.3 collective-permute-start.30
  588.4 17.2 %all-to-all-start.5 = ((f32[64,1,512]{2,1,0:T(1,128)}), f32[64,1,512]{2,1,0:T(1,128)S(1)}, u32[]{:S(2)}, u32[]{:S(2)}) async-start(f32[64,1,512]{2,1,0:T(1,128)} %reshape.599), calls=%async_computation.11 | async-start | bytes 262144 | tf_op jit(solution)/shard_map/all_to_all | solution.py:209
  612.3 5.3 all-to-all-done.5
  635.3 4.4 copy.288
  639.7 7.5 reshape.601
  647.2 6.9 all-to-all-start.6
  656.8 8.7 %all-to-all-done.6 = f32[64,1,512]{2,1,0:T(1,128)S(1)} async-done(((f32[64,1,512]{2,1,0:T(1,128)}), f32[64,1,512]{2,1,0:T(1,128)S(1)}, u32[]{:S(2)}, u32[]{:S(2)}) %all-to-all-start.6) | async-done | bytes 131104 | tf_op jit(solution)/shard_map/all_to_all | solution.py:173
  666.5 7.9 reshape.602
  674.4 5.4 copy.347
  679.9 4.6 fusion.189
  684.6 5.4 convolution_subtract_fusion
  702.5 6.5 collective-permute-start.35
  709.1 25.8 %all-reduce.19.cloned.1.call-done = f32[64,512]{1,0:T(8,128)} async-done(((f32[64,512]{1,0:T(8,128)}), f32[64,512]{1,0:T(8,128)}) %all-reduce.19.cloned.1.call-update) | async-done | bytes 131088 | tf_op jit(solution)/shard_map/psum | solution.py:178
  737.1 5.0 convolution_bitcast_fusion
  742.1 4.9 convolution_bitcast_fusion.1
  750.1 12.4 %reduce-scatter.23.cloned.1.call-done = f32[256,2,64]{0,2,1:T(8,128)} async-done(((f32[512,2,64]{0,2,1:T(8,128)}), f32[256,2,64]{0,2,1:T(8,128)}) %reduce-scatter.23.cloned.1.call-update) | async-done | bytes 131088 | tf_op jit(solution)/shard_map/reduce_scatter | solution.py:206
  764.5 12.3 %all-to-all-start.7 = ((f32[64,1,512]{2,1,0:T(1,128)}), f32[64,1,512]{2,1,0:T(1,128)S(1)}, u32[]{:S(2)}, u32[]{:S(2)}) async-start(f32[64,1,512]{2,1,0:T(1,128)} %reshape.603), calls=%async_computation.15 | async-start | bytes 262144 | tf_op jit(solution)/shard_map/all_to_all | solution.py:209
  783.2 5.7 all-to-all-done.7
  (413 shorter events, 261.2 us)
Async XLA Ops:
  8.4 44.1 %collective-permute-start.1 = (f32[1,4,2,512]{3,2,1,0:T(2,128)S(1)}, f32[1,4,2,512]{3,2,1,0:T(2,128)S(1)}, u32[]{:S(2)}, u32[]{:S(2)}) collective-permute-start(f32[1,4,2,512]{3,2,1,0:T(2,128)S(1)} %get-tuple-element.127), channel_id=1, source_target_pairs={{2,0},{4,2},{6,4},{8,6},{10,8},{12,10},{14,12},{16,14},{18,16},{20... | collective-permute-start | bytes 49160 | tf_op jit(solution)/shard_map/ppermute | solution.py:25
  9.7 42.8 %collective-permute-start.2 = (f32[1,4,2,512]{3,2,1,0:T(2,128)S(1)}, f32[1,4,2,512]{3,2,1,0:T(2,128)S(1)}, u32[]{:S(2)}, u32[]{:S(2)}) collective-permute-start(f32[1,4,2,512]{3,2,1,0:T(2,128)S(1)} %get-tuple-element.126), channel_id=1, source_target_pairs={{0,2},{2,4},{4,6},{6,8},{8,10},{10,12},{12,14},{14,16},{16,18},{18... | collective-permute-start | bytes 49160 | tf_op jit(solution)/shard_map/ppermute | solution.py:23
  33.9 34.6 %all-to-all-start = ((f32[64,1,512]{2,1,0:T(1,128)}), f32[64,1,512]{2,1,0:T(1,128)S(1)}, u32[]{:S(2)}, u32[]{:S(2)}) async-start(f32[64,1,512]{2,1,0:T(1,128)} %reshape.589), calls=%async_computation | async-start | bytes 262144 | tf_op jit(solution)/shard_map/all_to_all | solution.py:173
  52.5 62.6 %reduce-scatter.9.cloned.1.call-start = ((), (), s32[]{:S(2)}) async-start(), calls=%async_computation.16 | async-start | bytes 393216 | tf_op jit(solution)/shard_map/reduce_scatter | solution.py:177
  52.7 4.7 collective-permute-start.3
  56.1 3.3 collective-permute-start.4
  61.8 210.9 %copy-start.2 = (f32[1,1,4,64,512]{4,3,2,1,0:T(8,128)}, f32[1,1,4,64,512]{4,3,2,1,0:T(8,128)S(1)}, u32[]{:S(2)}) copy-start(f32[1,1,4,64,512]{4,3,2,1,0:T(8,128)S(1)} %get-tuple-element.113) | copy-start | bytes 1572868
  63.7 40.4 %collective-permute-start.5 = (f32[2,1,4,2,512]{4,3,2,1,0:T(2,128)}, f32[2,1,4,2,512]{4,3,2,1,0:T(2,128)S(1)}, u32[]{:S(2)}, u32[]{:S(2)}) collective-permute-start(f32[2,1,4,2,512]{4,3,2,1,0:T(2,128)} %get-tuple-element.98), channel_id=1, source_target_pairs={{0,2},{2,4},{4,6},{6,8},{8,10},{10,12},{12,14},{14,16},{16,18},{18... | collective-permute-start | bytes 98312 | tf_op jit(solution)/shard_map/ppermute | solution.py:23
  66.9 37.2 %collective-permute-start.6 = (f32[2,1,4,2,512]{4,3,2,1,0:T(2,128)}, f32[2,1,4,2,512]{4,3,2,1,0:T(2,128)S(1)}, u32[]{:S(2)}, u32[]{:S(2)}) collective-permute-start(f32[2,1,4,2,512]{4,3,2,1,0:T(2,128)} %get-tuple-element.99), channel_id=1, source_target_pairs={{2,0},{4,2},{6,4},{8,6},{10,8},{12,10},{14,12},{16,14},{18,16},{20... | collective-permute-start | bytes 98312 | tf_op jit(solution)/shard_map/ppermute | solution.py:25
  93.4 57.8 %all-reduce.13.cloned.1.call-start = ((), (), s32[]{:S(2)}) async-start(), calls=%async_computation.17 | async-start | bytes 262144 | tf_op jit(solution)/shard_map/psum | solution.py:178
  94.1 23.7 %collective-permute-start = (f32[64,512]{1,0:T(8,128)}, f32[64,512]{1,0:T(8,128)}, u32[]{:S(2)}, u32[]{:S(2)}) collective-permute-start(f32[64,512]{1,0:T(8,128)} %slice_bitcast_fusion.24), channel_id=1, source_target_pairs={{0,128},{128,0},{1,129},{129,1},{2,130},{130,2},{3,131},{131,3},{4... | collective-permute-start | bytes 393224 | tf_op jit(solution)/shard_map/ppermute | solution.py:33
  106.2 5.1 collective-permute-start.7
  107.4 4.6 collective-permute-start.8
  115.2 70.6 %reduce-scatter.11.cloned.1.call-start = ((), (), s32[]{:S(2)}) async-start(), calls=%async_computation.18 | async-start | bytes 393216 | tf_op jit(solution)/shard_map/reduce_scatter | solution.py:206
  168.7 5.3 collective-permute-start.10
  170.0 4.8 collective-permute-start.11
  175.6 8.3 %collective-permute-start.12 = (f32[1,4,68,2]{3,2,1,0:T(8,128)S(1)}, f32[1,4,68,2]{3,2,1,0:T(8,128)}, u32[]{:S(2)}, u32[]{:S(2)}) collective-permute-start(f32[1,4,68,2]{3,2,1,0:T(8,128)S(1)} %get-tuple-element.110), channel_id=1, source_target_pairs={{1,0},{3,2},{5,4},{7,6},{9,8},{11,10},{13,12},{15,14},{17,16},{19,... | collective-permute-start | bytes 6536 | tf_op jit(solution)/shard_map/ppermute | solution.py:25
  182.6 22.4 %collective-permute-start.13 = (f32[1,4,68,2]{3,2,1,0:T(8,128)}, f32[1,4,68,2]{3,2,1,0:T(8,128)}, u32[]{:S(2)}, u32[]{:S(2)}) collective-permute-start(f32[1,4,68,2]{3,2,1,0:T(8,128)} %get-tuple-element.111), channel_id=1, source_target_pairs={{0,1},{2,3},{4,5},{6,7},{8,9},{10,11},{12,13},{14,15},{16,17},{18,... | collective-permute-start | bytes 6536 | tf_op jit(solution)/shard_map/ppermute | solution.py:23
  187.7 28.6 %all-to-all-start.1 = ((f32[64,1,512]{2,1,0:T(1,128)}), f32[64,1,512]{2,1,0:T(1,128)S(1)}, u32[]{:S(2)}, u32[]{:S(2)}) async-start(f32[64,1,512]{2,1,0:T(1,128)} %reshape.591), calls=%async_computation.3 | async-start | bytes 262144 | tf_op jit(solution)/shard_map/all_to_all | solution.py:209
  268.0 16.0 %all-to-all-start.2 = ((f32[64,1,512]{2,1,0:T(1,128)}), f32[64,1,512]{2,1,0:T(1,128)S(1)}, u32[]{:S(2)}, u32[]{:S(2)}) async-start(f32[64,1,512]{2,1,0:T(1,128)} %reshape.593), calls=%async_computation.4 | async-start | bytes 262144 | tf_op jit(solution)/shard_map/all_to_all | solution.py:173
  272.6 52.8 %reduce-scatter.13.cloned.1.call-start = ((), (), s32[]{:S(2)}) async-start(), calls=%async_computation.19 | async-start | bytes 393216 | tf_op jit(solution)/shard_map/reduce_scatter | solution.py:177
  275.7 32.9 %collective-permute-start.14 = (f32[2,1,4,2,512]{4,3,2,1,0:T(2,128)S(1)}, f32[2,1,4,2,512]{4,3,2,1,0:T(2,128)S(1)}, u32[]{:S(2)}, u32[]{:S(2)}) collective-permute-start(f32[2,1,4,2,512]{4,3,2,1,0:T(2,128)S(1)} %get-tuple-element.96), channel_id=1, source_target_pairs={{0,2},{2,4},{4,6},{6,8},{8,10},{10,12},{12,14},{14,16},{16,18},{18... | collective-permute-start | bytes 98312 | tf_op jit(solution)/shard_map/ppermute | solution.py:23
  278.5 30.1 %collective-permute-start.15 = (f32[2,1,4,2,512]{4,3,2,1,0:T(2,128)S(1)}, f32[2,1,4,2,512]{4,3,2,1,0:T(2,128)S(1)}, u32[]{:S(2)}, u32[]{:S(2)}) collective-permute-start(f32[2,1,4,2,512]{4,3,2,1,0:T(2,128)S(1)} %get-tuple-element.97), channel_id=1, source_target_pairs={{2,0},{4,2},{6,4},{8,6},{10,8},{12,10},{14,12},{16,14},{18,16},{20... | collective-permute-start | bytes 98312 | tf_op jit(solution)/shard_map/ppermute | solution.py:25
  308.5 52.2 %all-reduce.15.cloned.1.call-start = ((), (), s32[]{:S(2)}) async-start(), calls=%async_computation.20 | async-start | bytes 262144 | tf_op jit(solution)/shard_map/psum | solution.py:178
  309.9 8.8 %collective-permute-start.16 = (f32[2,1,4,68,2]{4,3,2,1,0:T(8,128)S(1)}, f32[2,1,4,68,2]{4,3,2,1,0:T(8,128)S(1)}, u32[]{:S(2)}, u32[]{:S(2)}) collective-permute-start(f32[2,1,4,68,2]{4,3,2,1,0:T(8,128)S(1)} %get-tuple-element.88), channel_id=1, source_target_pairs={{0,1},{2,3},{4,5},{6,7},{8,9},{10,11},{12,13},{14,15},{16,17},{18,... | collective-permute-start | bytes 13064 | tf_op jit(solution)/shard_map/ppermute | solution.py:23
  311.2 7.5 collective-permute-start.17
  317.5 10.5 %collective-permute-start.9 = (f32[64,512]{1,0:T(8,128)S(1)}, f32[64,512]{1,0:T(8,128)S(1)}, u32[]{:S(2)}, u32[]{:S(2)}) collective-permute-start(f32[64,512]{1,0:T(8,128)S(1)} %slice_bitcast_fusion.19), channel_id=1, source_target_pairs={{0,128},{128,0},{1,129},{129,1},{2,130},{130,2},{3,131},{131,3},{4... | collective-permute-start | bytes 393224 | tf_op jit(solution)/shard_map/ppermute | solution.py:33
  325.5 73.1 %reduce-scatter.15.cloned.1.call-start = ((), (), s32[]{:S(2)}) async-start(), calls=%async_computation.21 | async-start | bytes 393216 | tf_op jit(solution)/shard_map/reduce_scatter | solution.py:206
  373.9 6.1 collective-permute-start.19
  375.2 4.8 collective-permute-start.20
  380.9 9.4 %collective-permute-start.21 = (f32[1,4,68,2]{3,2,1,0:T(8,128)S(1)}, f32[1,4,68,2]{3,2,1,0:T(8,128)S(1)}, u32[]{:S(2)}, u32[]{:S(2)}) collective-permute-start(f32[1,4,68,2]{3,2,1,0:T(8,128)S(1)} %get-tuple-element.106), channel_id=1, source_target_pairs={{1,0},{3,2},{5,4},{7,6},{9,8},{11,10},{13,12},{15,14},{17,16},{19,... | collective-permute-start | bytes 6536 | tf_op jit(solution)/shard_map/ppermute | solution.py:25
  388.8 26.0 %collective-permute-start.22 = (f32[1,4,68,2]{3,2,1,0:T(8,128)}, f32[1,4,68,2]{3,2,1,0:T(8,128)}, u32[]{:S(2)}, u32[]{:S(2)}) collective-permute-start(f32[1,4,68,2]{3,2,1,0:T(8,128)} %get-tuple-element.107), channel_id=1, source_target_pairs={{0,1},{2,3},{4,5},{6,7},{8,9},{10,11},{12,13},{14,15},{16,17},{18,... | collective-permute-start | bytes 6536 | tf_op jit(solution)/shard_map/ppermute | solution.py:23
  402.2 24.5 %all-to-all-start.3 = ((f32[64,1,512]{2,1,0:T(1,128)}), f32[64,1,512]{2,1,0:T(1,128)}, u32[]{:S(2)}, u32[]{:S(2)}) async-start(f32[64,1,512]{2,1,0:T(1,128)} %reshape.595), calls=%async_computation.7 | async-start | bytes 262144 | tf_op jit(solution)/shard_map/all_to_all | solution.py:209
  462.3 16.7 %all-to-all-start.4 = ((f32[64,1,512]{2,1,0:T(1,128)}), f32[64,1,512]{2,1,0:T(1,128)}, u32[]{:S(2)}, u32[]{:S(2)}) async-start(f32[64,1,512]{2,1,0:T(1,128)} %reshape.597), calls=%async_computation.8 | async-start | bytes 262144 | tf_op jit(solution)/shard_map/all_to_all | solution.py:173
  467.7 53.3 %reduce-scatter.17.cloned.1.call-start = ((), (), s32[]{:S(2)}) async-start(), calls=%async_computation.22 | async-start | bytes 393216 | tf_op jit(solution)/shard_map/reduce_scatter | solution.py:177
  471.8 32.9 %collective-permute-start.23 = (f32[2,1,4,2,512]{4,3,2,1,0:T(2,128)}, f32[2,1,4,2,512]{4,3,2,1,0:T(2,128)S(1)}, u32[]{:S(2)}, u32[]{:S(2)}) collective-permute-start(f32[2,1,4,2,512]{4,3,2,1,0:T(2,128)} %get-tuple-element.94), channel_id=1, source_target_pairs={{0,2},{2,4},{4,6},{6,8},{8,10},{10,12},{12,14},{14,16},{16,18},{18... | collective-permute-start | bytes 98312 | tf_op jit(solution)/shard_map/ppermute | solution.py:23
  474.6 30.2 %collective-permute-start.24 = (f32[2,1,4,2,512]{4,3,2,1,0:T(2,128)}, f32[2,1,4,2,512]{4,3,2,1,0:T(2,128)}, u32[]{:S(2)}, u32[]{:S(2)}) collective-permute-start(f32[2,1,4,2,512]{4,3,2,1,0:T(2,128)} %get-tuple-element.95), channel_id=1, source_target_pairs={{2,0},{4,2},{6,4},{8,6},{10,8},{12,10},{14,12},{16,14},{18,16},{20... | collective-permute-start | bytes 98312 | tf_op jit(solution)/shard_map/ppermute | solution.py:25
  504.7 51.8 %all-reduce.17.cloned.1.call-start = ((), (), s32[]{:S(2)}) async-start(), calls=%async_computation.23 | async-start | bytes 262144 | tf_op jit(solution)/shard_map/psum | solution.py:178
  506.1 7.4 collective-permute-start.25
  507.4 6.2 collective-permute-start.26
  512.7 11.0 %collective-permute-start.18 = (f32[64,512]{1,0:T(8,128)}, f32[64,512]{1,0:T(8,128)}, u32[]{:S(2)}, u32[]{:S(2)}) collective-permute-start(f32[64,512]{1,0:T(8,128)} %slice_bitcast_fusion.14), channel_id=1, source_target_pairs={{0,128},{128,0},{1,129},{129,1},{2,130},{130,2},{3,131},{131,3},{4... | collective-permute-start | bytes 393224 | tf_op jit(solution)/shard_map/ppermute | solution.py:33
  516.1 40.4 %copy-start.29 = (f32[64,512]{1,0:T(8,128)S(1)}, f32[64,512]{1,0:T(8,128)}, u32[]{:S(2)}) copy-start(f32[64,512]{1,0:T(8,128)} %param.21) | copy-start | bytes 393220
  516.1 40.4 %copy-start.36 = (f32[64,512]{1,0:T(8,128)S(1)}, f32[64,512]{1,0:T(8,128)}, u32[]{:S(2)}) copy-start(f32[64,512]{1,0:T(8,128)} %param.22) | copy-start | bytes 393220
  516.1 40.4 %copy-start.39 = (f32[64,512]{1,0:T(8,128)S(1)}, f32[64,512]{1,0:T(8,128)}, u32[]{:S(2)}) copy-start(f32[64,512]{1,0:T(8,128)} %copy-done.37) | copy-start | bytes 393220
  516.1 40.4 %copy-start.44 = (f32[64,512]{1,0:T(8,128)S(1)}, f32[64,512]{1,0:T(8,128)}, u32[]{:S(2)}) copy-start(f32[64,512]{1,0:T(8,128)} %copy-done.43) | copy-start | bytes 393220
  521.1 65.3 %reduce-scatter.19.cloned.1.call-start = ((), (), s32[]{:S(2)}) async-start(), calls=%async_computation.24 | async-start | bytes 393216 | tf_op jit(solution)/shard_map/reduce_scatter | solution.py:206
  574.1 5.4 collective-permute-start.28
  575.5 4.8 collective-permute-start.29
  581.2 29.3 %collective-permute-start.30 = (f32[1,4,68,2]{3,2,1,0:T(8,128)}, f32[1,4,68,2]{3,2,1,0:T(8,128)}, u32[]{:S(2)}, u32[]{:S(2)}) collective-permute-start(f32[1,4,68,2]{3,2,1,0:T(8,128)} %get-tuple-element.102), channel_id=1, source_target_pairs={{1,0},{3,2},{5,4},{7,6},{9,8},{11,10},{13,12},{15,14},{17,16},{19,... | collective-permute-start | bytes 6536 | tf_op jit(solution)/shard_map/ppermute | solution.py:25
  588.4 29.2 %all-to-all-start.5 = ((f32[64,1,512]{2,1,0:T(1,128)}), f32[64,1,512]{2,1,0:T(1,128)S(1)}, u32[]{:S(2)}, u32[]{:S(2)}) async-start(f32[64,1,512]{2,1,0:T(1,128)} %reshape.599), calls=%async_computation.11 | async-start | bytes 262144 | tf_op jit(solution)/shard_map/all_to_all | solution.py:209
  609.2 45.0 %collective-permute-start.31 = (f32[1,4,68,2]{3,2,1,0:T(8,128)}, f32[1,4,68,2]{3,2,1,0:T(8,128)}, u32[]{:S(2)}, u32[]{:S(2)}) collective-permute-start(f32[1,4,68,2]{3,2,1,0:T(8,128)} %get-tuple-element.103), channel_id=1, source_target_pairs={{0,1},{2,3},{4,5},{6,7},{8,9},{10,11},{12,13},{14,15},{16,17},{18,... | collective-permute-start | bytes 6536 | tf_op jit(solution)/shard_map/ppermute | solution.py:23
  647.2 18.4 %all-to-all-start.6 = ((f32[64,1,512]{2,1,0:T(1,128)}), f32[64,1,512]{2,1,0:T(1,128)S(1)}, u32[]{:S(2)}, u32[]{:S(2)}) async-start(f32[64,1,512]{2,1,0:T(1,128)} %reshape.601), calls=%async_computation.12 | async-start | bytes 262144 | tf_op jit(solution)/shard_map/all_to_all | solution.py:173
  654.1 45.3 %reduce-scatter.21.cloned.1.call-start = ((), (), s32[]{:S(2)}) async-start(), calls=%async_computation.25 | async-start | bytes 393216 | tf_op jit(solution)/shard_map/reduce_scatter | solution.py:177
  690.0 44.9 %all-reduce.19.cloned.1.call-start = ((), (), s32[]{:S(2)}) async-start(), calls=%async_computation.26 | async-start | bytes 262144 | tf_op jit(solution)/shard_map/psum | solution.py:178
  693.1 41.8 %copy-start.30 = (f32[64,512]{1,0:T(8,128)S(1)}, f32[64,512]{1,0:T(8,128)}, u32[]{:S(2)}) copy-start(f32[64,512]{1,0:T(8,128)} %param.21) | copy-start | bytes 393220
  693.1 41.8 %copy-start.46 = (f32[64,512]{1,0:T(8,128)S(1)}, f32[64,512]{1,0:T(8,128)}, u32[]{:S(2)}) copy-start(f32[64,512]{1,0:T(8,128)} %copy-done.45) | copy-start | bytes 393220
  693.2 41.8 %copy-start.47 = (f32[64,512]{1,0:T(8,128)S(1)}, f32[64,512]{1,0:T(8,128)}, u32[]{:S(2)}) copy-start(f32[64,512]{1,0:T(8,128)} %get-tuple-element.71) | copy-start | bytes 393220
  693.2 6.3 collective-permute-start.32
  695.6 4.7 collective-permute-start.33
  696.9 12.1 %collective-permute-start.27 = (f32[64,512]{1,0:T(8,128)S(1)}, f32[64,512]{1,0:T(8,128)S(1)}, u32[]{:S(2)}, u32[]{:S(2)}) collective-permute-start(f32[64,512]{1,0:T(8,128)S(1)} %slice_bitcast_fusion.9), channel_id=1, source_target_pairs={{0,128},{128,0},{1,129},{129,1},{2,130},{130,2},{3,131},{131,3},{4... | collective-permute-start | bytes 393224 | tf_op jit(solution)/shard_map/ppermute | solution.py:33
  699.5 63.0 %reduce-scatter.23.cloned.1.call-start = ((), (), s32[]{:S(2)}) async-start(), calls=%async_computation.27 | async-start | bytes 393216 | tf_op jit(solution)/shard_map/reduce_scatter | solution.py:206
  701.2 46.5 %collective-permute-start.34 = (f32[2,1,4,68,2]{4,3,2,1,0:T(8,128)}, f32[2,1,4,68,2]{4,3,2,1,0:T(8,128)S(1)}, u32[]{:S(2)}, u32[]{:S(2)}) collective-permute-start(f32[2,1,4,68,2]{4,3,2,1,0:T(8,128)} %get-tuple-element.84), channel_id=1, source_target_pairs={{0,1},{2,3},{4,5},{6,7},{8,9},{10,11},{12,13},{14,15},{16,17},{18,... | collective-permute-start | bytes 13064 | tf_op jit(solution)/shard_map/ppermute | solution.py:23
  702.5 45.2 %collective-permute-start.35 = (f32[2,1,4,68,2]{4,3,2,1,0:T(8,128)}, f32[2,1,4,68,2]{4,3,2,1,0:T(8,128)S(1)}, u32[]{:S(2)}, u32[]{:S(2)}) collective-permute-start(f32[2,1,4,68,2]{4,3,2,1,0:T(8,128)} %get-tuple-element.85), channel_id=1, source_target_pairs={{1,0},{3,2},{5,4},{7,6},{9,8},{11,10},{13,12},{15,14},{17,16},{19,... | collective-permute-start | bytes 13064 | tf_op jit(solution)/shard_map/ppermute | solution.py:25
  764.5 24.4 %all-to-all-start.7 = ((f32[64,1,512]{2,1,0:T(1,128)}), f32[64,1,512]{2,1,0:T(1,128)S(1)}, u32[]{:S(2)}, u32[]{:S(2)}) async-start(f32[64,1,512]{2,1,0:T(1,128)} %reshape.603), calls=%async_computation.15 | async-start | bytes 262144 | tf_op jit(solution)/shard_map/all_to_all | solution.py:209
  (42 other events, 520.2 us)
Sparse Core Ops, SparseCore 0:
  93.5 17.6 reduce-scatter.8
  115.3 35.8 all-reduce.12
  164.1 14.6 reduce-scatter.10
  308.6 16.7 reduce-scatter.12
  327.8 32.8 all-reduce.14
  380.1 18.4 reduce-scatter.14
  504.8 16.1 reduce-scatter.16
  523.6 32.8 all-reduce.16
  569.5 14.6 reduce-scatter.18
  690.1 9.2 reduce-scatter.20
  702.0 32.8 all-reduce.18
  747.8 14.6 reduce-scatter.22
where the time goes:
time: 815 us; the launch traced here: 804 us
  waiting for transfers between devices  205 us (25%)
  starting transfers between devices  197 us (24%)
  local copies, waits for them, and re-layouts  159 us (20%)
  matrix products  123 us (15%)
  other arithmetic  104 us (13%)
  between operations  16.4 us (2%)
    psum x4, waiting for transfers between devices, per_device(): relief = lax.psum(own_depth, 'grp') * scale_back  125 us
    unnamed x116, local copies, waits for them, and re-layouts  73.8 us
    all_to_all x4, starting transfers between devices, per_device(): lax.all_to_all(by_modes, 'gx', split_axis=0, concat_axis=2, tiled=True)  59.3 us
    ppermute x16, starting transfers between devices, extended(): lax.ppermute(head, axis, [((i + 1) % count, i) for i in range(ends)])  50.3 us
    ppermute x16, starting transfers between devices, extended(): lax.ppermute(tail, axis, [(i, (i + 1) % count) for i in range(ends)])  38.2 us
    all_to_all x4, starting transfers between devices, per_device(): lax.all_to_all(in_space, 'gx', split_axis=2, concat_axis=0, tiled=True)  35.7 us
    all_to_all x4, waiting for transfers between devices, per_device(): lax.all_to_all(by_modes, 'gx', split_axis=0, concat_axis=2, tiled=True)  27.6 us
    all_to_all x9, local copies, waits for them, and re-layouts, per_device(): lax.all_to_all(in_space, 'gx', split_axis=2, concat_axis=0, tiled=True)  22.7 us
  transfers between devices with their start and end apart: 56, of which 22 were waited for; matrix products, arithmetic and copies ran while one was open for 28% of the time, Pallas kernels for 0%

commit v1 on v0

--- a/solution.py
+++ b/solution.py
@@ -170,7 +170,10 @@
     for step_number in range(NSTEP):
         summed = jnp.sum(weights[:, :, None, :] * lagged, axis=0)
         in_space = strike_inverse(summed, strike_devices, strike_rows)
-        by_rows = lax.all_to_all(in_space, "gx", split_axis=2, concat_axis=0, tiled=True)
+        by_rows = jnp.concatenate(
+            lax.all_to_all(jnp.stack(jnp.split(in_space, lax.axis_size("gx"), axis=2)), "gx", 0, 0),
+            axis=0,
+        )
         partial_value = jnp.einsum(
             "jy,jz->yz", by_rows[:, 0], back_cos, precision=FULL_PRECISION
         ) - jnp.einsum("jy,jz->yz", by_rows[:, 1], back_sin, precision=FULL_PRECISION)

time: 815 us -> 724 us (0.89)
  local copies, waits for them, and re-layouts: 159 us -> 75.1 us
  starting transfers between devices: 197 us -> 187 us
    unnamed x116 -> x374, local copies, waits for them, and re-layouts: 73.8 us -> 28.2 us
    all_to_all x9 -> x5, local copies, waits for them, and re-layouts: 22.7 us -> 0.77 us  [per_device(): lax.all_to_all(jnp.stack(jnp.split(in_space, lax.axis_size('gx'), axis=2)...]
    another operation x12, local copies, waits for them, and re-layouts: 22.5 us -> 10.7 us  [strike_inverse(): jnp.stack([real_part.reshape(planes_count, total_count), imag_part.reshap...]
    ppermute x4, starting transfers between devices: 12.7 us -> 2.77 us  [from_partner(): lax.ppermute(x, axis, [(i, i ^ 1 << stride) for i in range(lax.axis_size(...]
  transfers between devices with their start and end apart: 56 -> 56, of which waited for: 22 -> 23; matrix products, arithmetic and copies ran while one was open for 28% -> 24% of each run, Pallas kernels for 0% -> 0%
where the time goes in v1:
time: 724 us; the launch traced here: 715 us
  waiting for transfers between devices  210 us (29%)
  starting transfers between devices  187 us (26%)
  matrix products  127 us (18%)
  other arithmetic  98.6 us (14%)
  local copies, waits for them, and re-layouts  75.1 us (10%)
  between operations  16.6 us (2%)
    psum x4, waiting for transfers between devices, per_device(): relief = lax.psum(own_depth, 'grp') * scale_back  123 us
    all_to_all x4, starting transfers between devices, per_device(): lax.all_to_all(by_modes, 'gx', split_axis=0, concat_axis=2, tiled=True)  59.1 us
    ppermute x16, starting transfers between devices, extended(): lax.ppermute(head, axis, [((i + 1) % count, i) for i in range(ends)])  51 us
    ppermute x16, starting transfers between devices, extended(): lax.ppermute(tail, axis, [(i, (i + 1) % count) for i in range(ends)])  38.3 us
    all_to_all x4, starting transfers between devices, per_device(): lax.all_to_all(jnp.stack(jnp.split(in_space, lax.axis_size('gx'), axis=2)...  35.1 us
    unnamed x374, local copies, waits for them, and re-layouts  28.2 us
    all_to_all x4, waiting for transfers between devices, per_device(): lax.all_to_all(by_modes, 'gx', split_axis=0, concat_axis=2, tiled=True)  27.6 us
    dot_general x4, matrix products, per_device(): jnp.einsum('jy,jz->yz', by_rows[:, 1], back_sin, precision=FULL_PRECISION)  21.5 us
  transfers between devices with their start and end apart: 56, of which 23 were waited for; matrix products, arithmetic and copies ran while one was open for 24% of the time, Pallas kernels for 0%

profile of v1, /device:TPU:1, one launch (start us, length us, event | category | flops | bytes accessed | tf_op | source)
XLA Modules:
  0.0 714.8 jit_solution(5860039635598680984)
XLA Ops:
  9.7 4.6 collective-permute-start.2
  25.8 18.5 %all-to-all-start = ((f32[64,1,512]{2,1,0:T(1,128)}), f32[64,1,512]{2,1,0:T(1,128)S(1)}, u32[]{:S(2)}, u32[]{:S(2)}) async-start(f32[64,1,512]{2,1,0:T(1,128)} %reshape.605), calls=%async_computation | async-start | bytes 262144 | tf_op jit(solution)/shard_map/all_to_all | solution.py:174
  44.5 3.6 collective-permute-start.3
  54.6 3.2 collective-permute-start.5
  62.7 4.6 fusion.195
  67.3 5.4 convolution_subtract_fusion.3
  77.4 3.8 collective-permute-start.8
  82.0 3.1 pad_maximum_fusion.3
  85.1 5.3 reduce-scatter.9.cloned.1.call-done
  93.5 32.4 %all-reduce.13.cloned.1.call-done = f32[64,512]{1,0:T(8,128)} async-done(((f32[64,512]{1,0:T(8,128)}), f32[64,512]{1,0:T(8,128)}) %all-reduce.13.cloned.1.call-update) | async-done | bytes 131088 | tf_op jit(solution)/shard_map/psum | solution.py:181
  128.1 5.0 convolution_bitcast_fusion.6
  133.1 4.9 convolution_bitcast_fusion.7
  138.7 5.1 fusion.70
  145.2 4.0 collective-permute-start.11
  150.8 5.0 collective-permute-start.12
  162.7 17.2 %all-to-all-start.1 = ((f32[64,1,512]{2,1,0:T(1,128)}), f32[64,1,512]{2,1,0:T(1,128)S(1)}, u32[]{:S(2)}, u32[]{:S(2)}) async-start(f32[64,1,512]{2,1,0:T(1,128)} %reshape.607), calls=%async_computation.3 | async-start | bytes 262144 | tf_op jit(solution)/shard_map/all_to_all | solution.py:212
  179.9 3.4 fusion.51
  183.3 8.0 %all-to-all-done.1 = f32[64,1,512]{2,1,0:T(1,128)S(1)} async-done(((f32[64,1,512]{2,1,0:T(1,128)}), f32[64,1,512]{2,1,0:T(1,128)S(1)}, u32[]{:S(2)}, u32[]{:S(2)}) %all-to-all-start.1) | async-done | bytes 131104 | tf_op jit(solution)/shard_map/all_to_all | solution.py:212
  235.2 5.0 all-to-all-start.2
  243.3 2.8 collective-permute-start.14
  247.4 4.2 all-to-all-done.2
  252.8 4.6 fusion.193
  257.4 5.4 convolution_subtract_fusion.2
  265.5 6.3 collective-permute-start.17
  275.1 4.6 reduce-scatter.13.cloned.1.call-done
  282.4 32.7 %all-reduce.15.cloned.1.call-done = f32[64,512]{1,0:T(8,128)} async-done(((f32[64,512]{1,0:T(8,128)}), f32[64,512]{1,0:T(8,128)}) %all-reduce.15.cloned.1.call-update) | async-done | bytes 131088 | tf_op jit(solution)/shard_map/psum | solution.py:181
  317.2 5.0 convolution_bitcast_fusion.4
  322.3 4.9 convolution_bitcast_fusion.5
  329.6 4.0 collective-permute-start.20
  335.2 4.6 collective-permute-start.21
  339.8 3.6 fusion.6
  345.7 7.2 %reduce-scatter.15.cloned.1.call-done = f32[256,2,64]{0,2,1:T(8,128)} async-done(((f32[512,2,64]{0,2,1:T(8,128)}), f32[256,2,64]{0,2,1:T(8,128)}) %reduce-scatter.15.cloned.1.call-update) | async-done | bytes 131088 | tf_op jit(solution)/shard_map/reduce_scatter | solution.py:209
  354.9 12.3 %all-to-all-start.3 = ((f32[64,1,512]{2,1,0:T(1,128)}), f32[64,1,512]{2,1,0:T(1,128)S(1)}, u32[]{:S(2)}, u32[]{:S(2)}) async-start(f32[64,1,512]{2,1,0:T(1,128)} %reshape.611), calls=%async_computation.7 | async-start | bytes 262144 | tf_op jit(solution)/shard_map/all_to_all | solution.py:212
  367.3 3.3 fusion.46
  370.6 8.7 %all-to-all-done.3 = f32[64,1,512]{2,1,0:T(1,128)S(1)} async-done(((f32[64,1,512]{2,1,0:T(1,128)}), f32[64,1,512]{2,1,0:T(1,128)S(1)}, u32[]{:S(2)}, u32[]{:S(2)}) %all-to-all-start.3) | async-done | bytes 131104 | tf_op jit(solution)/shard_map/all_to_all | solution.py:212
  402.5 4.7 all-to-all-start.4
  410.7 2.9 collective-permute-start.23
  415.1 3.5 all-to-all-done.4
  419.8 4.6 fusion.191
  424.5 5.4 convolution_subtract_fusion.1
  432.6 4.8 collective-permute-start.26
  440.4 5.4 reduce-scatter.17.cloned.1.call-done
  448.7 32.6 %all-reduce.17.cloned.1.call-done = f32[64,512]{1,0:T(8,128)} async-done(((f32[64,512]{1,0:T(8,128)}), f32[64,512]{1,0:T(8,128)}) %all-reduce.17.cloned.1.call-update) | async-done | bytes 131088 | tf_op jit(solution)/shard_map/psum | solution.py:181
  483.6 5.0 convolution_bitcast_fusion.2
  488.5 4.9 convolution_bitcast_fusion.3
  494.2 4.5 fusion.102
  500.1 4.0 collective-permute-start.29
  505.7 5.3 collective-permute-start.30
  513.0 17.2 %all-to-all-start.5 = ((f32[64,1,512]{2,1,0:T(1,128)}), f32[64,1,512]{2,1,0:T(1,128)S(1)}, u32[]{:S(2)}, u32[]{:S(2)}) async-start(f32[64,1,512]{2,1,0:T(1,128)} %reshape.615), calls=%async_computation.11 | async-start | bytes 262144 | tf_op jit(solution)/shard_map/all_to_all | solution.py:212
  530.3 3.5 fusion.5
  537.0 5.3 all-to-all-done.5
  571.5 6.9 all-to-all-start.6
  581.1 8.7 %all-to-all-done.6 = f32[64,1,512]{2,1,0:T(1,128)S(1)} async-done(((f32[64,1,512]{2,1,0:T(1,128)}), f32[64,1,512]{2,1,0:T(1,128)S(1)}, u32[]{:S(2)}, u32[]{:S(2)}) %all-to-all-start.6) | async-done | bytes 131104 | tf_op jit(solution)/shard_map/all_to_all | solution.py:174
  591.1 4.6 fusion.189
  595.7 5.4 convolution_subtract_fusion
  601.2 2.9 fusion.32
  613.4 6.8 collective-permute-start.35
  620.2 25.8 %all-reduce.19.cloned.1.call-done = f32[64,512]{1,0:T(8,128)} async-done(((f32[64,512]{1,0:T(8,128)}), f32[64,512]{1,0:T(8,128)}) %all-reduce.19.cloned.1.call-update) | async-done | bytes 131088 | tf_op jit(solution)/shard_map/psum | solution.py:181
  648.2 5.0 convolution_bitcast_fusion
  653.2 4.9 convolution_bitcast_fusion.1
  661.2 12.4 %reduce-scatter.23.cloned.1.call-done = f32[256,2,64]{0,2,1:T(8,128)} async-done(((f32[512,2,64]{0,2,1:T(8,128)}), f32[256,2,64]{0,2,1:T(8,128)}) %reduce-scatter.23.cloned.1.call-update) | async-done | bytes 131088 | tf_op jit(solution)/shard_map/reduce_scatter | solution.py:209
  675.6 12.3 %all-to-all-start.7 = ((f32[64,1,512]{2,1,0:T(1,128)}), f32[64,1,512]{2,1,0:T(1,128)S(1)}, u32[]{:S(2)}, u32[]{:S(2)}) async-start(f32[64,1,512]{2,1,0:T(1,128)} %reshape.619), calls=%async_computation.15 | async-start | bytes 262144 | tf_op jit(solution)/shard_map/all_to_all | solution.py:212
  688.0 3.8 fusion.119
  694.4 5.6 all-to-all-done.7
  (667 shorter events, 223.2 us)
Async XLA Ops:
  8.4 35.9 %collective-permute-start.1 = (f32[1,4,2,512]{3,2,1,0:T(2,128)S(1)}, f32[1,4,2,512]{3,2,1,0:T(2,128)S(1)}, u32[]{:S(2)}, u32[]{:S(2)}) collective-permute-start(f32[1,4,2,512]{3,2,1,0:T(2,128)S(1)} %get-tuple-element.127), channel_id=1, source_target_pairs={{2,0},{4,2},{6,4},{8,6},{10,8},{12,10},{14,12},{16,14},{18,16},{20... | collective-permute-start | bytes 49160 | tf_op jit(solution)/shard_map/ppermute | solution.py:25
  9.7 34.6 %collective-permute-start.2 = (f32[1,4,2,512]{3,2,1,0:T(2,128)S(1)}, f32[1,4,2,512]{3,2,1,0:T(2,128)S(1)}, u32[]{:S(2)}, u32[]{:S(2)}) collective-permute-start(f32[1,4,2,512]{3,2,1,0:T(2,128)S(1)} %get-tuple-element.126), channel_id=1, source_target_pairs={{0,2},{2,4},{4,6},{6,8},{8,10},{10,12},{12,14},{14,16},{16,18},{18... | collective-permute-start | bytes 49160 | tf_op jit(solution)/shard_map/ppermute | solution.py:23
  25.8 33.6 %all-to-all-start = ((f32[64,1,512]{2,1,0:T(1,128)}), f32[64,1,512]{2,1,0:T(1,128)S(1)}, u32[]{:S(2)}, u32[]{:S(2)}) async-start(f32[64,1,512]{2,1,0:T(1,128)} %reshape.605), calls=%async_computation | async-start | bytes 262144 | tf_op jit(solution)/shard_map/all_to_all | solution.py:174
  44.3 46.2 %reduce-scatter.9.cloned.1.call-start = ((), (), s32[]{:S(2)}) async-start(), calls=%async_computation.16 | async-start | bytes 393216 | tf_op jit(solution)/shard_map/reduce_scatter | solution.py:180
  44.5 4.9 collective-permute-start.3
  48.1 3.3 collective-permute-start.4
  52.7 187.6 %copy-start.2 = (f32[1,1,4,64,512]{4,3,2,1,0:T(8,128)}, f32[1,1,4,64,512]{4,3,2,1,0:T(8,128)S(1)}, u32[]{:S(2)}) copy-start(f32[1,1,4,64,512]{4,3,2,1,0:T(8,128)S(1)} %get-tuple-element.113) | copy-start | bytes 1572868
  54.6 19.5 %collective-permute-start.5 = (f32[2,1,4,2,512]{4,3,2,1,0:T(2,128)}, f32[2,1,4,2,512]{4,3,2,1,0:T(2,128)S(1)}, u32[]{:S(2)}, u32[]{:S(2)}) collective-permute-start(f32[2,1,4,2,512]{4,3,2,1,0:T(2,128)} %get-tuple-element.98), channel_id=1, source_target_pairs={{0,2},{2,4},{4,6},{6,8},{8,10},{10,12},{12,14},{14,16},{16,18},{18... | collective-permute-start | bytes 98312 | tf_op jit(solution)/shard_map/ppermute | solution.py:23
  57.8 16.3 %collective-permute-start.6 = (f32[2,1,4,2,512]{4,3,2,1,0:T(2,128)}, f32[2,1,4,2,512]{4,3,2,1,0:T(2,128)S(1)}, u32[]{:S(2)}, u32[]{:S(2)}) collective-permute-start(f32[2,1,4,2,512]{4,3,2,1,0:T(2,128)} %get-tuple-element.99), channel_id=1, source_target_pairs={{2,0},{4,2},{6,4},{8,6},{10,8},{12,10},{14,12},{16,14},{18,16},{20... | collective-permute-start | bytes 98312 | tf_op jit(solution)/shard_map/ppermute | solution.py:25
  72.7 53.2 %all-reduce.13.cloned.1.call-start = ((), (), s32[]{:S(2)}) async-start(), calls=%async_computation.17 | async-start | bytes 262144 | tf_op jit(solution)/shard_map/psum | solution.py:181
  73.4 20.1 %collective-permute-start = (f32[64,512]{1,0:T(8,128)}, f32[64,512]{1,0:T(8,128)}, u32[]{:S(2)}, u32[]{:S(2)}) collective-permute-start(f32[64,512]{1,0:T(8,128)} %slice_bitcast_fusion.24), channel_id=1, source_target_pairs={{0,128},{128,0},{1,129},{129,1},{2,130},{130,2},{3,131},{131,3},{4... | collective-permute-start | bytes 393224 | tf_op jit(solution)/shard_map/ppermute | solution.py:33
  76.2 5.1 collective-permute-start.7
  77.4 4.6 collective-permute-start.8
  90.5 70.3 %reduce-scatter.11.cloned.1.call-start = ((), (), s32[]{:S(2)}) async-start(), calls=%async_computation.18 | async-start | bytes 393216 | tf_op jit(solution)/shard_map/reduce_scatter | solution.py:209
  143.9 5.3 collective-permute-start.10
  145.2 4.8 collective-permute-start.11
  150.8 8.0 %collective-permute-start.12 = (f32[1,4,68,2]{3,2,1,0:T(8,128)S(1)}, f32[1,4,68,2]{3,2,1,0:T(8,128)}, u32[]{:S(2)}, u32[]{:S(2)}) collective-permute-start(f32[1,4,68,2]{3,2,1,0:T(8,128)S(1)} %get-tuple-element.110), channel_id=1, source_target_pairs={{1,0},{3,2},{5,4},{7,6},{9,8},{11,10},{13,12},{15,14},{17,16},{19,... | collective-permute-start | bytes 6536 | tf_op jit(solution)/shard_map/ppermute | solution.py:25
  157.5 22.4 %collective-permute-start.13 = (f32[1,4,68,2]{3,2,1,0:T(8,128)}, f32[1,4,68,2]{3,2,1,0:T(8,128)}, u32[]{:S(2)}, u32[]{:S(2)}) collective-permute-start(f32[1,4,68,2]{3,2,1,0:T(8,128)} %get-tuple-element.111), channel_id=1, source_target_pairs={{0,1},{2,3},{4,5},{6,7},{8,9},{10,11},{12,13},{14,15},{16,17},{18,... | collective-permute-start | bytes 6536 | tf_op jit(solution)/shard_map/ppermute | solution.py:23
  162.7 28.6 %all-to-all-start.1 = ((f32[64,1,512]{2,1,0:T(1,128)}), f32[64,1,512]{2,1,0:T(1,128)S(1)}, u32[]{:S(2)}, u32[]{:S(2)}) async-start(f32[64,1,512]{2,1,0:T(1,128)} %reshape.607), calls=%async_computation.3 | async-start | bytes 262144 | tf_op jit(solution)/shard_map/all_to_all | solution.py:212
  235.2 16.4 %all-to-all-start.2 = ((f32[64,1,512]{2,1,0:T(1,128)}), f32[64,1,512]{2,1,0:T(1,128)S(1)}, u32[]{:S(2)}, u32[]{:S(2)}) async-start(f32[64,1,512]{2,1,0:T(1,128)} %reshape.609), calls=%async_computation.4 | async-start | bytes 262144 | tf_op jit(solution)/shard_map/all_to_all | solution.py:174
  240.2 39.6 %reduce-scatter.13.cloned.1.call-start = ((), (), s32[]{:S(2)}) async-start(), calls=%async_computation.19 | async-start | bytes 393216 | tf_op jit(solution)/shard_map/reduce_scatter | solution.py:180
  243.3 19.6 %collective-permute-start.14 = (f32[2,1,4,2,512]{4,3,2,1,0:T(2,128)S(1)}, f32[2,1,4,2,512]{4,3,2,1,0:T(2,128)S(1)}, u32[]{:S(2)}, u32[]{:S(2)}) collective-permute-start(f32[2,1,4,2,512]{4,3,2,1,0:T(2,128)S(1)} %get-tuple-element.96), channel_id=1, source_target_pairs={{0,2},{2,4},{4,6},{6,8},{8,10},{10,12},{12,14},{14,16},{16,18},{18... | collective-permute-start | bytes 98312 | tf_op jit(solution)/shard_map/ppermute | solution.py:23
  246.1 16.8 %collective-permute-start.15 = (f32[2,1,4,2,512]{4,3,2,1,0:T(2,128)S(1)}, f32[2,1,4,2,512]{4,3,2,1,0:T(2,128)S(1)}, u32[]{:S(2)}, u32[]{:S(2)}) collective-permute-start(f32[2,1,4,2,512]{4,3,2,1,0:T(2,128)S(1)} %get-tuple-element.97), channel_id=1, source_target_pairs={{2,0},{4,2},{6,4},{8,6},{10,8},{12,10},{14,12},{16,14},{18,16},{20... | collective-permute-start | bytes 98312 | tf_op jit(solution)/shard_map/ppermute | solution.py:25
  262.8 52.2 %all-reduce.15.cloned.1.call-start = ((), (), s32[]{:S(2)}) async-start(), calls=%async_computation.20 | async-start | bytes 262144 | tf_op jit(solution)/shard_map/psum | solution.py:181
  264.2 9.1 %collective-permute-start.16 = (f32[2,1,4,68,2]{4,3,2,1,0:T(8,128)S(1)}, f32[2,1,4,68,2]{4,3,2,1,0:T(8,128)S(1)}, u32[]{:S(2)}, u32[]{:S(2)}) collective-permute-start(f32[2,1,4,68,2]{4,3,2,1,0:T(8,128)S(1)} %get-tuple-element.88), channel_id=1, source_target_pairs={{0,1},{2,3},{4,5},{6,7},{8,9},{10,11},{12,13},{14,15},{16,17},{18,... | collective-permute-start | bytes 13064 | tf_op jit(solution)/shard_map/ppermute | solution.py:23
  265.5 7.8 %collective-permute-start.17 = (f32[2,1,4,68,2]{4,3,2,1,0:T(8,128)S(1)}, f32[2,1,4,68,2]{4,3,2,1,0:T(8,128)S(1)}, u32[]{:S(2)}, u32[]{:S(2)}) collective-permute-start(f32[2,1,4,68,2]{4,3,2,1,0:T(8,128)S(1)} %get-tuple-element.89), channel_id=1, source_target_pairs={{1,0},{3,2},{5,4},{7,6},{9,8},{11,10},{13,12},{15,14},{17,16},{19,... | collective-permute-start | bytes 13064 | tf_op jit(solution)/shard_map/ppermute | solution.py:25
  272.5 9.9 %collective-permute-start.9 = (f32[64,512]{1,0:T(8,128)}, f32[64,512]{1,0:T(8,128)S(1)}, u32[]{:S(2)}, u32[]{:S(2)}) collective-permute-start(f32[64,512]{1,0:T(8,128)} %slice_bitcast_fusion.19), channel_id=1, source_target_pairs={{0,128},{128,0},{1,129},{129,1},{2,130},{130,2},{3,131},{131,3},{4... | collective-permute-start | bytes 393224 | tf_op jit(solution)/shard_map/ppermute | solution.py:33
  279.8 73.1 %reduce-scatter.15.cloned.1.call-start = ((), (), s32[]{:S(2)}) async-start(), calls=%async_computation.21 | async-start | bytes 393216 | tf_op jit(solution)/shard_map/reduce_scatter | solution.py:209
  328.3 6.1 collective-permute-start.19
  329.6 4.8 collective-permute-start.20
  335.2 9.6 %collective-permute-start.21 = (f32[1,4,68,2]{3,2,1,0:T(8,128)S(1)}, f32[1,4,68,2]{3,2,1,0:T(8,128)S(1)}, u32[]{:S(2)}, u32[]{:S(2)}) collective-permute-start(f32[1,4,68,2]{3,2,1,0:T(8,128)S(1)} %get-tuple-element.106), channel_id=1, source_target_pairs={{1,0},{3,2},{5,4},{7,6},{9,8},{11,10},{13,12},{15,14},{17,16},{19,... | collective-permute-start | bytes 6536 | tf_op jit(solution)/shard_map/ppermute | solution.py:25
  343.4 23.9 %collective-permute-start.22 = (f32[1,4,68,2]{3,2,1,0:T(8,128)}, f32[1,4,68,2]{3,2,1,0:T(8,128)}, u32[]{:S(2)}, u32[]{:S(2)}) collective-permute-start(f32[1,4,68,2]{3,2,1,0:T(8,128)} %get-tuple-element.107), channel_id=1, source_target_pairs={{0,1},{2,3},{4,5},{6,7},{8,9},{10,11},{12,13},{14,15},{16,17},{18,... | collective-permute-start | bytes 6536 | tf_op jit(solution)/shard_map/ppermute | solution.py:23
  354.9 24.4 %all-to-all-start.3 = ((f32[64,1,512]{2,1,0:T(1,128)}), f32[64,1,512]{2,1,0:T(1,128)S(1)}, u32[]{:S(2)}, u32[]{:S(2)}) async-start(f32[64,1,512]{2,1,0:T(1,128)} %reshape.611), calls=%async_computation.7 | async-start | bytes 262144 | tf_op jit(solution)/shard_map/all_to_all | solution.py:212
  402.5 16.1 %all-to-all-start.4 = ((f32[64,1,512]{2,1,0:T(1,128)}), f32[64,1,512]{2,1,0:T(1,128)S(1)}, u32[]{:S(2)}, u32[]{:S(2)}) async-start(f32[64,1,512]{2,1,0:T(1,128)} %reshape.613), calls=%async_computation.8 | async-start | bytes 262144 | tf_op jit(solution)/shard_map/all_to_all | solution.py:174
  407.2 38.7 %reduce-scatter.17.cloned.1.call-start = ((), (), s32[]{:S(2)}) async-start(), calls=%async_computation.22 | async-start | bytes 393216 | tf_op jit(solution)/shard_map/reduce_scatter | solution.py:180
  410.7 19.3 %collective-permute-start.23 = (f32[2,1,4,2,512]{4,3,2,1,0:T(2,128)S(1)}, f32[2,1,4,2,512]{4,3,2,1,0:T(2,128)S(1)}, u32[]{:S(2)}, u32[]{:S(2)}) collective-permute-start(f32[2,1,4,2,512]{4,3,2,1,0:T(2,128)S(1)} %get-tuple-element.94), channel_id=1, source_target_pairs={{0,2},{2,4},{4,6},{6,8},{8,10},{10,12},{12,14},{14,16},{16,18},{18... | collective-permute-start | bytes 98312 | tf_op jit(solution)/shard_map/ppermute | solution.py:23
  413.6 16.3 %collective-permute-start.24 = (f32[2,1,4,2,512]{4,3,2,1,0:T(2,128)S(1)}, f32[2,1,4,2,512]{4,3,2,1,0:T(2,128)S(1)}, u32[]{:S(2)}, u32[]{:S(2)}) collective-permute-start(f32[2,1,4,2,512]{4,3,2,1,0:T(2,128)S(1)} %get-tuple-element.95), channel_id=1, source_target_pairs={{2,0},{4,2},{6,4},{8,6},{10,8},{12,10},{14,12},{16,14},{18,16},{20... | collective-permute-start | bytes 98312 | tf_op jit(solution)/shard_map/ppermute | solution.py:25
  429.9 51.4 %all-reduce.17.cloned.1.call-start = ((), (), s32[]{:S(2)}) async-start(), calls=%async_computation.23 | async-start | bytes 262144 | tf_op jit(solution)/shard_map/psum | solution.py:181
  431.3 7.4 %collective-permute-start.25 = (f32[2,1,4,68,2]{4,3,2,1,0:T(8,128)S(1)}, f32[2,1,4,68,2]{4,3,2,1,0:T(8,128)S(1)}, u32[]{:S(2)}, u32[]{:S(2)}) collective-permute-start(f32[2,1,4,68,2]{4,3,2,1,0:T(8,128)S(1)} %get-tuple-element.86), channel_id=1, source_target_pairs={{0,1},{2,3},{4,5},{6,7},{8,9},{10,11},{12,13},{14,15},{16,17},{18,... | collective-permute-start | bytes 13064 | tf_op jit(solution)/shard_map/ppermute | solution.py:23
  432.6 6.1 collective-permute-start.26
  438.0 10.7 %collective-permute-start.18 = (f32[64,512]{1,0:T(8,128)}, f32[64,512]{1,0:T(8,128)}, u32[]{:S(2)}, u32[]{:S(2)}) collective-permute-start(f32[64,512]{1,0:T(8,128)} %slice_bitcast_fusion.14), channel_id=1, source_target_pairs={{0,128},{128,0},{1,129},{129,1},{2,130},{130,2},{3,131},{131,3},{4... | collective-permute-start | bytes 393224 | tf_op jit(solution)/shard_map/ppermute | solution.py:33
  440.4 40.9 %copy-start.30 = (f32[64,512]{1,0:T(8,128)S(1)}, f32[64,512]{1,0:T(8,128)}, u32[]{:S(2)}) copy-start(f32[64,512]{1,0:T(8,128)} %param.21) | copy-start | bytes 393220
  440.4 40.9 %copy-start.37 = (f32[64,512]{1,0:T(8,128)S(1)}, f32[64,512]{1,0:T(8,128)}, u32[]{:S(2)}) copy-start(f32[64,512]{1,0:T(8,128)} %param.22) | copy-start | bytes 393220
  440.4 40.9 %copy-start.40 = (f32[64,512]{1,0:T(8,128)S(1)}, f32[64,512]{1,0:T(8,128)}, u32[]{:S(2)}) copy-start(f32[64,512]{1,0:T(8,128)} %copy-done.38) | copy-start | bytes 393220
  440.4 40.9 %copy-start.45 = (f32[64,512]{1,0:T(8,128)S(1)}, f32[64,512]{1,0:T(8,128)}, u32[]{:S(2)}) copy-start(f32[64,512]{1,0:T(8,128)} %copy-done.44) | copy-start | bytes 393220
  445.9 65.2 %reduce-scatter.19.cloned.1.call-start = ((), (), s32[]{:S(2)}) async-start(), calls=%async_computation.24 | async-start | bytes 393216 | tf_op jit(solution)/shard_map/reduce_scatter | solution.py:209
  498.7 5.4 collective-permute-start.28
  500.1 4.8 collective-permute-start.29
  505.7 29.3 %collective-permute-start.30 = (f32[1,4,68,2]{3,2,1,0:T(8,128)}, f32[1,4,68,2]{3,2,1,0:T(8,128)}, u32[]{:S(2)}, u32[]{:S(2)}) collective-permute-start(f32[1,4,68,2]{3,2,1,0:T(8,128)} %get-tuple-element.102), channel_id=1, source_target_pairs={{1,0},{3,2},{5,4},{7,6},{9,8},{11,10},{13,12},{15,14},{17,16},{19,... | collective-permute-start | bytes 6536 | tf_op jit(solution)/shard_map/ppermute | solution.py:25
  513.0 29.2 %all-to-all-start.5 = ((f32[64,1,512]{2,1,0:T(1,128)}), f32[64,1,512]{2,1,0:T(1,128)S(1)}, u32[]{:S(2)}, u32[]{:S(2)}) async-start(f32[64,1,512]{2,1,0:T(1,128)} %reshape.615), calls=%async_computation.11 | async-start | bytes 262144 | tf_op jit(solution)/shard_map/all_to_all | solution.py:212
  533.8 44.7 %collective-permute-start.31 = (f32[1,4,68,2]{3,2,1,0:T(8,128)}, f32[1,4,68,2]{3,2,1,0:T(8,128)}, u32[]{:S(2)}, u32[]{:S(2)}) collective-permute-start(f32[1,4,68,2]{3,2,1,0:T(8,128)} %get-tuple-element.103), channel_id=1, source_target_pairs={{0,1},{2,3},{4,5},{6,7},{8,9},{10,11},{12,13},{14,15},{16,17},{18,... | collective-permute-start | bytes 6536 | tf_op jit(solution)/shard_map/ppermute | solution.py:23
  571.5 18.4 %all-to-all-start.6 = ((f32[64,1,512]{2,1,0:T(1,128)}), f32[64,1,512]{2,1,0:T(1,128)S(1)}, u32[]{:S(2)}, u32[]{:S(2)}) async-start(f32[64,1,512]{2,1,0:T(1,128)} %reshape.617), calls=%async_computation.12 | async-start | bytes 262144 | tf_op jit(solution)/shard_map/all_to_all | solution.py:174
  578.4 32.2 %reduce-scatter.21.cloned.1.call-start = ((), (), s32[]{:S(2)}) async-start(), calls=%async_computation.25 | async-start | bytes 393216 | tf_op jit(solution)/shard_map/reduce_scatter | solution.py:180
  601.1 44.9 %all-reduce.19.cloned.1.call-start = ((), (), s32[]{:S(2)}) async-start(), calls=%async_computation.26 | async-start | bytes 262144 | tf_op jit(solution)/shard_map/psum | solution.py:181
  604.1 42.0 %copy-start.31 = (f32[64,512]{1,0:T(8,128)S(1)}, f32[64,512]{1,0:T(8,128)}, u32[]{:S(2)}) copy-start(f32[64,512]{1,0:T(8,128)} %param.21) | copy-start | bytes 393220
  604.1 42.0 %copy-start.47 = (f32[64,512]{1,0:T(8,128)S(1)}, f32[64,512]{1,0:T(8,128)}, u32[]{:S(2)}) copy-start(f32[64,512]{1,0:T(8,128)} %copy-done.46) | copy-start | bytes 393220
  604.1 42.0 %copy-start.48 = (f32[64,512]{1,0:T(8,128)S(1)}, f32[64,512]{1,0:T(8,128)}, u32[]{:S(2)}) copy-start(f32[64,512]{1,0:T(8,128)} %get-tuple-element.71) | copy-start | bytes 393220
  604.1 6.5 collective-permute-start.32
  606.5 4.7 collective-permute-start.33
  607.9 12.3 %collective-permute-start.27 = (f32[64,512]{1,0:T(8,128)S(1)}, f32[64,512]{1,0:T(8,128)S(1)}, u32[]{:S(2)}, u32[]{:S(2)}) collective-permute-start(f32[64,512]{1,0:T(8,128)S(1)} %slice_bitcast_fusion.9), channel_id=1, source_target_pairs={{0,128},{128,0},{1,129},{129,1},{2,130},{130,2},{3,131},{131,3},{4... | collective-permute-start | bytes 393224 | tf_op jit(solution)/shard_map/ppermute | solution.py:33
  610.6 63.1 %reduce-scatter.23.cloned.1.call-start = ((), (), s32[]{:S(2)}) async-start(), calls=%async_computation.27 | async-start | bytes 393216 | tf_op jit(solution)/shard_map/reduce_scatter | solution.py:209
  612.1 46.7 %collective-permute-start.34 = (f32[2,1,4,68,2]{4,3,2,1,0:T(8,128)}, f32[2,1,4,68,2]{4,3,2,1,0:T(8,128)S(1)}, u32[]{:S(2)}, u32[]{:S(2)}) collective-permute-start(f32[2,1,4,68,2]{4,3,2,1,0:T(8,128)} %get-tuple-element.84), channel_id=1, source_target_pairs={{0,1},{2,3},{4,5},{6,7},{8,9},{10,11},{12,13},{14,15},{16,17},{18,... | collective-permute-start | bytes 13064 | tf_op jit(solution)/shard_map/ppermute | solution.py:23
  613.4 45.4 %collective-permute-start.35 = (f32[2,1,4,68,2]{4,3,2,1,0:T(8,128)}, f32[2,1,4,68,2]{4,3,2,1,0:T(8,128)S(1)}, u32[]{:S(2)}, u32[]{:S(2)}) collective-permute-start(f32[2,1,4,68,2]{4,3,2,1,0:T(8,128)} %get-tuple-element.85), channel_id=1, source_target_pairs={{1,0},{3,2},{5,4},{7,6},{9,8},{11,10},{13,12},{15,14},{17,16},{19,... | collective-permute-start | bytes 13064 | tf_op jit(solution)/shard_map/ppermute | solution.py:25
  675.6 24.4 %all-to-all-start.7 = ((f32[64,1,512]{2,1,0:T(1,128)}), f32[64,1,512]{2,1,0:T(1,128)S(1)}, u32[]{:S(2)}, u32[]{:S(2)}) async-start(f32[64,1,512]{2,1,0:T(1,128)} %reshape.619), calls=%async_computation.15 | async-start | bytes 262144 | tf_op jit(solution)/shard_map/all_to_all | solution.py:212
  (43 other events, 587.7 us)
Sparse Core Ops, SparseCore 0:
  72.8 17.5 reduce-scatter.8
  93.0 32.8 all-reduce.12
  138.8 14.6 reduce-scatter.10
  263.0 16.7 reduce-scatter.12
  282.2 32.8 all-reduce.14
  334.5 18.4 reduce-scatter.14
  430.0 15.8 reduce-scatter.16
  448.4 32.8 all-reduce.16
  494.3 14.6 reduce-scatter.18
  601.2 9.2 reduce-scatter.20
  613.1 32.8 all-reduce.18
  658.9 14.6 reduce-scatter.22
